TPU v7x, 32 devices: a whole 2x2x4 slice. The times are simulated.
32 devices in a mesh: dp: 16 (over z, y, core), ctx: 2 (over x).
Axes of the slice: x: 2, y: 2, z: 4, core: 2. Of those that a mesh axis runs over, the one named last changes fastest.
Arguments:
- conv_input: bfloat16 [16, 256, 4096], P('dp', 'ctx'), may hold values from -6 to 6
- gate_value: bfloat16 [16, 256, 4096], P('dp', 'ctx'), may hold values from -6 to 6
- out_grad: bfloat16 [16, 256, 4096], P('dp', 'ctx'), may hold values from -6 to 6
- filter_taps: bfloat16 [128, 4096], P('dp'), may hold values from -0.5 to 0.5
Outputs:
- input_grad: bfloat16 [16, 256, 4096], P('dp', 'ctx')
- filter_grad: float32 [128, 4096], P('dp')
All inputs are finite; a program needn't handle non-finite values.
Results may differ from a plain program's by a relative error of at most 0.0051.
Values may be sent and summed in bfloat16 or wider, within the bound.
A program may use at most 64 MiB of HBM per device.

v0:
```python
import math
import jax
import jax.numpy as jnp
from jax import lax
from jax.sharding import PartitionSpec as P

TAPS = 128


def from_behind(block, axis, distance):
    devices = range(lax.axis_size(axis))
    route = [(i - distance, i) for i in devices if i - distance in devices]
    return lax.ppermute(block, axis, route)


def correlate(signal, kernel):
    return lax.conv_general_dilated(
        signal[None],
        kernel[:, None, :],
        (1,),
        "VALID",
        dimension_numbers=("NWC", "WIO", "NWC"),
        feature_group_count=signal.shape[1],
        preferred_element_type=jnp.float32,
    )[0]


def shards(conv_input, gate_value, out_grad, filter_taps):
    inputs = conv_input[0]
    rows = inputs.shape[0]
    mixed = (out_grad[0].astype(jnp.float32) * gate_value[0].astype(jnp.float32)).astype(
        jnp.bfloat16
    )
    rim_rows = from_behind(mixed[: TAPS - 1], "ctx", -1)
    grad_ext = jnp.concatenate([mixed, rim_rows], 0)
    partial_grad = correlate(grad_ext, inputs)
    full_taps = lax.all_gather(filter_taps, "dp", axis=0, tiled=True)
    back_sum = correlate(grad_ext, full_taps)
    summed = lax.psum(partial_grad, "ctx")
    shard_grad = lax.psum_scatter(summed, "dp", scatter_dimension=0, tiled=True)
    tokens_all = rows * lax.axis_size("ctx") * lax.axis_size("dp")
    scale_factor = 1.0 / math.sqrt(tokens_all)
    return (back_sum.astype(jnp.bfloat16)[None], shard_grad * scale_factor)


def solution(mesh):
    in_specs = (P("dp", "ctx", None), P("dp", "ctx", None), P("dp", "ctx", None), P("dp", None))
    out_specs = (P("dp", "ctx", None), P("dp", None))
    return jax.shard_map(shards, mesh=mesh, in_specs=in_specs, out_specs=out_specs, check_vma=False)
```

profile of v0, /device:TPU:0, one launch (start us, length us, event | category | flops | bytes accessed | tf_op | source)
XLA Modules:
  0.0 211.5 jit_solution(7849527368872966788)
XLA Ops:
  7.2 0.0 copy-start
  7.2 0.0 reduce-scatter.2.cloned.1.call-start
  7.2 1.9 multiply_convert_fusion
  9.2 0.1 slice_bitcast_fusion
  9.2 1.3 collective-permute-start
  10.5 26.2 %collective-permute-done = bf16[127,4096]{1,0:T(8,128)(2,1)S(1)} collective-permute-done((bf16[127,4096]{1,0:T(8,128)(2,1)S(1)}, bf16[127,4096]{1,0:T(8,128)(2,1)S(1)}, u32[]{:S(2)}, u32[]{:S(2)}) %collective-permute-start) | collective-permute-done | bytes 1040416 | tf_op jit(solution)/shard_map/ppermute | solution.py:13
  36.7 0.2 maximum_bitcast_fusion
  36.9 0.0 copy-done
  36.9 30.1 %fusion = f32[1,128,4096]{2,0,1:T(1,128)S(1)} fusion(bf16[1,255,4096]{2,1,0:T(8,128)(2,1)S(1)} %maximum_bitcast_fusion, bf16[128,1,4096]{2,0,1:T(8,128)(2,1)S(1)} %bitcast.10), kind=kOutput, calls=%fused_computation.1 | convolution fusion | flops 134217728 | bytes 5234688 | tf_op jit(solution)/shard_map/conv_general_dilated | solution.py:17
  67.0 3.0 %copy.23 = f32[1,128,4096]{2,1,0:T(8,128)} copy(f32[1,128,4096]{2,0,1:T(1,128)S(1)} %fusion) | data formatting | bytes 4194304
  70.0 0.0 reduce-scatter.2.cloned.1.call-update
  70.0 0.0 all-gather.2.cloned.1.call-start
  70.1 0.7 all-gather.2.cloned.1.call-update
  70.8 0.0 all-reduce.2.cloned.1.call-start
  70.8 62.3 %reduce-scatter.2.cloned.1.call-done = f32[8,4096]{1,0:T(8,128)} async-done(((f32[128,4096]{1,0:T(8,128)}), f32[8,4096]{1,0:T(8,128)}) %reduce-scatter.2.cloned.1.call-update) | async-done | bytes 131088 | tf_op jit(solution)/shard_map/reduce_scatter | solution.py:40
  133.1 0.0 all-reduce.2.cloned.1.call-update
  133.2 39.0 %all-gather.2.cloned.1.call-done = bf16[128,4096]{1,0:T(8,128)(2,1)} async-done(((bf16[8,4096]{1,0:T(8,128)(2,1)}), bf16[128,4096]{1,0:T(8,128)(2,1)}) %all-gather.2.cloned.1.call-update) | async-done | bytes 1048592 | tf_op jit(solution)/shard_map/all_gather | solution.py:37
  172.2 29.1 %convolution_convert_fusion = bf16[1,128,4096]{2,0,1:T(2,128)(2,1)S(1)} fusion(bf16[1,255,4096]{2,1,0:T(8,128)(2,1)S(1)} %maximum_bitcast_fusion, bf16[128,1,4096]{2,0,1:T(8,128)(2,1)} %bitcast.13), kind=kOutput, calls=%fused_computation | convolution fusion | flops 134742016 | bytes 4186112 | tf_op jit(solution)/shard_map/conv_general_dilated | solution.py:17
  201.3 2.1 copy.12
  203.4 0.0 all-reduce.2.cloned.1.call-done
  203.4 1.6 broadcast_multiply_fusion
Async XLA Ops:
  7.2 29.8 %copy-start = (bf16[1,128,4096]{2,1,0:T(8,128)(2,1)S(1)}, bf16[1,128,4096]{2,1,0:T(8,128)(2,1)}, u32[]{:S(2)}) copy-start(bf16[1,128,4096]{2,1,0:T(8,128)(2,1)} %param.4) | copy-start | bytes 3145732
  7.2 126.0 %reduce-scatter.2.cloned.1.call-start = ((), (), s32[]{:S(2)}) async-start(), calls=%async_computation.2 | async-start | bytes 2228224 | tf_op jit(solution)/shard_map/reduce_scatter | solution.py:40
  9.2 27.5 %collective-permute-start = (bf16[127,4096]{1,0:T(8,128)(2,1)S(1)}, bf16[127,4096]{1,0:T(8,128)(2,1)S(1)}, u32[]{:S(2)}, u32[]{:S(2)}) collective-permute-start(bf16[127,4096]{1,0:T(8,128)(2,1)S(1)} %slice_bitcast_fusion), channel_id=1, source_target_pairs={{1,0},{3,2},{5,4},{7,6},{9,8},{11,10},{13,12},{15,14},{17,16},{19,... | collective-permute-start | bytes 3121160 | tf_op jit(solution)/shard_map/ppermute | solution.py:13
  70.0 102.1 %all-gather.2.cloned.1.call-start = ((), (), s32[]{:S(2)}) async-start(), calls=%async_computation.1 | async-start | bytes 1114112 | tf_op jit(solution)/shard_map/all_gather | solution.py:37
  70.8 132.6 %all-reduce.2.cloned.1.call-start = ((), (), s32[]{:S(2)}) async-start(), calls=%async_computation.3 | async-start | bytes 262144 | tf_op jit(solution)/shard_map/psum | solution.py:39
Sparse Core Ops, SparseCore 0:
  70.2 62.9 reduce-scatter.1
  135.3 36.8 all-gather.1
  174.4 20.4 all-reduce.1
where the time goes:
time: 212 us; the launch traced here: 211 us
  waiting for transfers between devices  128 us (60%)
  matrix products  59.2 us (28%)
  between operations  13.8 us (7%)
  local copies, waits for them, and re-layouts  5.18 us (2%)
  other arithmetic  3.71 us (2%)
    reduce_scatter x1, waiting for transfers between devices, shards(): shard_grad = lax.psum_scatter(summed, 'dp', scatter_dimension=0, tiled=True)  62.3 us
    conv_general_dilated x2, matrix products, correlate(): lax.conv_general_dilated(signal[None], kernel[:, None, :], (1,), 'VALID',...  59.2 us
    all_gather x1, waiting for transfers between devices, shards(): full_taps = lax.all_gather(filter_taps, 'dp', axis=0, tiled=True)  39 us
    ppermute x1, waiting for transfers between devices, from_behind(): return lax.ppermute(block, axis, route)  26.2 us
    unnamed x4, local copies, waits for them, and re-layouts  5.1 us
  transfers between devices with their start and end apart: 4, of which 3 were waited for; matrix products, arithmetic and copies ran while one was open for 15% of the time, Pallas kernels for 0%

commit v1 on v0

--- a/solution.py
+++ b/solution.py
@@ -34,7 +34,12 @@
     rim_rows = from_behind(mixed[: TAPS - 1], "ctx", -1)
     grad_ext = jnp.concatenate([mixed, rim_rows], 0)
     partial_grad = correlate(grad_ext, inputs)
-    full_taps = lax.all_gather(filter_taps, "dp", axis=0, tiled=True)
+    ring = [filter_taps]
+    for hop in range(15):
+        ring.append(lax.ppermute(ring[-1], "dp", [(dev, (dev + 1) % 16) for dev in range(16)]))
+    full_taps = jnp.roll(
+        jnp.concatenate(ring[::-1], axis=0), (lax.axis_index("dp") + 1) * ring[0].shape[0], axis=0
+    )
     back_sum = correlate(grad_ext, full_taps)
     summed = lax.psum(partial_grad, "ctx")
     shard_grad = lax.psum_scatter(summed, "dp", scatter_dimension=0, tiled=True)

time: 212 us -> 259 us (1.22)
  waiting for transfers between devices: 128 us -> 156 us
  local copies, waits for them, and re-layouts: 5.18 us -> 21.5 us
    ppermute x0 -> x15, waiting for transfers between devices: none -> 93.6 us  [shards(): lax.ppermute(ring[-1], 'dp', [(dev, (dev + 1) % 16) for dev in range(16)])]
    all_gather x1 -> x0, waiting for transfers between devices: 39 us -> none  [shards(): full_taps = lax.all_gather(filter_taps, 'dp', axis=0, tiled=True)]
    ppermute x1, waiting for transfers between devices: 26.2 us -> 4.95 us  [from_behind(): return lax.ppermute(block, axis, route)]
    unnamed x4 -> x75, local copies, waits for them, and re-layouts: 5.1 us -> 18.5 us
    reduce_scatter x1, waiting for transfers between devices: 62.3 us -> 57.4 us  [shards(): shard_grad = lax.psum_scatter(summed, 'dp', scatter_dimension=0, tiled=True)]
  transfers between devices with their start and end apart: 4 -> 18, of which waited for: 3 -> 17; matrix products, arithmetic and copies ran while one was open for 15% -> 19% of each run, Pallas kernels for 0% -> 0%
where the time goes in v1:
time: 259 us; the launch traced here: 258 us
  waiting for transfers between devices  156 us (60%)
  matrix products  59.2 us (23%)
  local copies, waits for them, and re-layouts  21.5 us (8%)
  between operations  14.5 us (6%)
  other arithmetic  4.76 us (2%)
    ppermute x15, waiting for transfers between devices, shards(): lax.ppermute(ring[-1], 'dp', [(dev, (dev + 1) % 16) for dev in range(16)])  93.6 us
    conv_general_dilated x2, matrix products, correlate(): lax.conv_general_dilated(signal[None], kernel[:, None, :], (1,), 'VALID',...  59.2 us
    reduce_scatter x1, waiting for transfers between devices, shards(): shard_grad = lax.psum_scatter(summed, 'dp', scatter_dimension=0, tiled=True)  57.4 us
    unnamed x75, local copies, waits for them, and re-layouts  18.5 us
  transfers between devices with their start and end apart: 18, of which 17 were waited for; matrix products, arithmetic and copies ran while one was open for 19% of the time, Pallas kernels for 0%

profile of v1, /device:TPU:0, one launch (start us, length us, event | category | flops | bytes accessed | tf_op | source)
XLA Modules:
  0.0 258.0 jit_solution(8226032722990518492)
XLA Ops:
  7.2 0.0 copy-start
  7.2 0.0 reduce-scatter.2.cloned.1.call-start
  7.2 0.5 collective-permute-start.1
  7.8 7.1 %collective-permute-done.1 = bf16[8,4096]{1,0:T(8,128)(2,1)S(1)} collective-permute-done((bf16[8,4096]{1,0:T(8,128)(2,1)}, bf16[8,4096]{1,0:T(8,128)(2,1)S(1)}, u32[]{:S(2)}, u32[]{:S(2)}) %collective-permute-start.1) | collective-permute-done | bytes 65568 | tf_op jit(solution)/shard_map/ppermute | solution.py:39
  14.9 0.0 collective-permute-start.2
  14.9 6.4 %collective-permute-done.2 = bf16[8,4096]{1,0:T(8,128)(2,1)S(1)} collective-permute-done((bf16[8,4096]{1,0:T(8,128)(2,1)S(1)}, bf16[8,4096]{1,0:T(8,128)(2,1)S(1)}, u32[]{:S(2)}, u32[]{:S(2)}) %collective-permute-start.2) | collective-permute-done | bytes 65568 | tf_op jit(solution)/shard_map/ppermute | solution.py:39
  21.3 0.0 collective-permute-start.3
  21.3 6.4 %collective-permute-done.3 = bf16[8,4096]{1,0:T(8,128)(2,1)S(1)} collective-permute-done((bf16[8,4096]{1,0:T(8,128)(2,1)S(1)}, bf16[8,4096]{1,0:T(8,128)(2,1)S(1)}, u32[]{:S(2)}, u32[]{:S(2)}) %collective-permute-start.3) | collective-permute-done | bytes 65568 | tf_op jit(solution)/shard_map/ppermute | solution.py:39
  27.7 0.0 collective-permute-start.4
  27.7 6.4 %collective-permute-done.4 = bf16[8,4096]{1,0:T(8,128)(2,1)S(1)} collective-permute-done((bf16[8,4096]{1,0:T(8,128)(2,1)S(1)}, bf16[8,4096]{1,0:T(8,128)(2,1)S(1)}, u32[]{:S(2)}, u32[]{:S(2)}) %collective-permute-start.4) | collective-permute-done | bytes 65568 | tf_op jit(solution)/shard_map/ppermute | solution.py:39
  34.1 0.0 collective-permute-start.5
  34.1 6.4 %collective-permute-done.5 = bf16[8,4096]{1,0:T(8,128)(2,1)S(1)} collective-permute-done((bf16[8,4096]{1,0:T(8,128)(2,1)S(1)}, bf16[8,4096]{1,0:T(8,128)(2,1)S(1)}, u32[]{:S(2)}, u32[]{:S(2)}) %collective-permute-start.5) | collective-permute-done | bytes 65568 | tf_op jit(solution)/shard_map/ppermute | solution.py:39
  40.5 0.0 collective-permute-start.6
  40.5 6.4 %collective-permute-done.6 = bf16[8,4096]{1,0:T(8,128)(2,1)S(1)} collective-permute-done((bf16[8,4096]{1,0:T(8,128)(2,1)S(1)}, bf16[8,4096]{1,0:T(8,128)(2,1)S(1)}, u32[]{:S(2)}, u32[]{:S(2)}) %collective-permute-start.6) | collective-permute-done | bytes 65568 | tf_op jit(solution)/shard_map/ppermute | solution.py:39
  46.9 6.4 %collective-permute-done.7 = bf16[8,4096]{1,0:T(8,128)(2,1)S(1)} collective-permute-done((bf16[8,4096]{1,0:T(8,128)(2,1)S(1)}, bf16[8,4096]{1,0:T(8,128)(2,1)S(1)}, u32[]{:S(2)}, u32[]{:S(2)}) %collective-permute-start.7) | collective-permute-done | bytes 65568 | tf_op jit(solution)/shard_map/ppermute | solution.py:39
  53.2 0.0 collective-permute-start.8
  53.3 6.4 %collective-permute-done.8 = bf16[8,4096]{1,0:T(8,128)(2,1)S(1)} collective-permute-done((bf16[8,4096]{1,0:T(8,128)(2,1)S(1)}, bf16[8,4096]{1,0:T(8,128)(2,1)S(1)}, u32[]{:S(2)}, u32[]{:S(2)}) %collective-permute-start.8) | collective-permute-done | bytes 65568 | tf_op jit(solution)/shard_map/ppermute | solution.py:39
  59.6 6.4 %collective-permute-done.9 = bf16[8,4096]{1,0:T(8,128)(2,1)S(1)} collective-permute-done((bf16[8,4096]{1,0:T(8,128)(2,1)S(1)}, bf16[8,4096]{1,0:T(8,128)(2,1)S(1)}, u32[]{:S(2)}, u32[]{:S(2)}) %collective-permute-start.9) | collective-permute-done | bytes 65568 | tf_op jit(solution)/shard_map/ppermute | solution.py:39
  66.0 6.4 %collective-permute-done.10 = bf16[8,4096]{1,0:T(8,128)(2,1)S(1)} collective-permute-done((bf16[8,4096]{1,0:T(8,128)(2,1)S(1)}, bf16[8,4096]{1,0:T(8,128)(2,1)S(1)}, u32[]{:S(2)}, u32[]{:S(2)}) %collective-permute-start.10) | collective-permute-done | bytes 65568 | tf_op jit(solution)/shard_map/ppermute | solution.py:39
  72.4 0.0 collective-permute-start.11
  72.4 6.4 %collective-permute-done.11 = bf16[8,4096]{1,0:T(8,128)(2,1)S(1)} collective-permute-done((bf16[8,4096]{1,0:T(8,128)(2,1)S(1)}, bf16[8,4096]{1,0:T(8,128)(2,1)S(1)}, u32[]{:S(2)}, u32[]{:S(2)}) %collective-permute-start.11) | collective-permute-done | bytes 65568 | tf_op jit(solution)/shard_map/ppermute | solution.py:39
  78.8 0.0 collective-permute-start.12
  78.8 6.4 %collective-permute-done.12 = bf16[8,4096]{1,0:T(8,128)(2,1)S(1)} collective-permute-done((bf16[8,4096]{1,0:T(8,128)(2,1)S(1)}, bf16[8,4096]{1,0:T(8,128)(2,1)S(1)}, u32[]{:S(2)}, u32[]{:S(2)}) %collective-permute-start.12) | collective-permute-done | bytes 65568 | tf_op jit(solution)/shard_map/ppermute | solution.py:39
  85.2 6.4 %collective-permute-done.13 = bf16[8,4096]{1,0:T(8,128)(2,1)S(1)} collective-permute-done((bf16[8,4096]{1,0:T(8,128)(2,1)S(1)}, bf16[8,4096]{1,0:T(8,128)(2,1)S(1)}, u32[]{:S(2)}, u32[]{:S(2)}) %collective-permute-start.13) | collective-permute-done | bytes 65568 | tf_op jit(solution)/shard_map/ppermute | solution.py:39
  91.6 0.0 copy-start.19
  91.6 0.1 collective-permute-start.14
  91.7 1.8 multiply_convert_fusion
  93.5 0.0 copy-start.4
  93.5 4.7 %collective-permute-done.14 = bf16[8,4096]{1,0:T(8,128)(2,1)} collective-permute-done((bf16[8,4096]{1,0:T(8,128)(2,1)S(1)}, bf16[8,4096]{1,0:T(8,128)(2,1)}, u32[]{:S(2)}, u32[]{:S(2)}) %collective-permute-start.14) | collective-permute-done | bytes 65568 | tf_op jit(solution)/shard_map/ppermute | solution.py:39
  98.2 0.1 slice_bitcast_fusion
  98.3 1.3 collective-permute-start
  99.6 0.0 copy-start.20
  99.6 0.0 copy-start.18
  99.7 5.2 %collective-permute-done.15 = bf16[8,4096]{1,0:T(8,128)(2,1)} collective-permute-done((bf16[8,4096]{1,0:T(8,128)(2,1)}, bf16[8,4096]{1,0:T(8,128)(2,1)}, u32[]{:S(2)}, u32[]{:S(2)}) %collective-permute-start.15) | collective-permute-done | bytes 65568 | tf_op jit(solution)/shard_map/ppermute | solution.py:39
  104.9 0.8 constant_dynamic-update-slice_fusion.31
  105.7 0.8 constant_dynamic-update-slice_fusion.30
  106.6 0.8 constant_dynamic-update-slice_fusion.29
  107.4 0.8 constant_dynamic-update-slice_fusion.28
  108.3 0.8 constant_dynamic-update-slice_fusion.27
  109.1 0.8 constant_dynamic-update-slice_fusion.26
  110.0 0.8 constant_dynamic-update-slice_fusion.25
  110.8 0.8 constant_dynamic-update-slice_fusion.24
  111.6 0.8 constant_dynamic-update-slice_fusion.23
  112.5 0.8 constant_dynamic-update-slice_fusion.22
  113.4 0.8 constant_dynamic-update-slice_fusion.15
  114.3 0.8 constant_dynamic-update-slice_fusion.14
  115.3 5.0 %collective-permute-done = bf16[127,4096]{1,0:T(8,128)(2,1)} collective-permute-done((bf16[127,4096]{1,0:T(8,128)(2,1)S(1)}, bf16[127,4096]{1,0:T(8,128)(2,1)}, u32[]{:S(2)}, u32[]{:S(2)}) %collective-permute-start) | collective-permute-done | bytes 1040416 | tf_op jit(solution)/shard_map/ppermute | solution.py:13
  120.3 1.4 maximum_bitcast_fusion
  121.7 30.1 %fusion = f32[1,128,4096]{2,0,1:T(1,128)S(1)} fusion(bf16[1,255,4096]{2,1,0:T(8,128)(2,1)S(1)} %maximum_bitcast_fusion, bf16[128,1,4096]{2,0,1:T(8,128)(2,1)S(1)} %bitcast.11), kind=kOutput, calls=%fused_computation.1 | convolution fusion | flops 134217728 | bytes 5234688 | tf_op jit(solution)/shard_map/conv_general_dilated | solution.py:17
  151.8 3.0 %copy.23 = f32[1,128,4096]{2,1,0:T(8,128)} copy(f32[1,128,4096]{2,0,1:T(1,128)S(1)} %fusion) | data formatting | bytes 4194304
  154.8 0.0 reduce-scatter.2.cloned.1.call-update
  154.8 0.0 all-reduce.2.cloned.1.call-start
  154.9 0.6 constant_dynamic-update-slice_fusion.5
  155.5 0.6 constant_dynamic-update-slice_fusion.4
  156.1 0.6 constant_dynamic-update-slice_fusion.3
  156.8 0.6 constant_dynamic-update-slice_fusion.2
  157.4 0.6 constant_dynamic-update-slice_fusion.1
  158.0 0.6 constant_dynamic-update-slice_fusion
  158.6 2.3 dynamic-slice_bitcast_fusion
  160.9 57.4 %reduce-scatter.2.cloned.1.call-done = f32[8,4096]{1,0:T(8,128)} async-done(((f32[128,4096]{1,0:T(8,128)}), f32[8,4096]{1,0:T(8,128)}) %reduce-scatter.2.cloned.1.call-update) | async-done | bytes 131088 | tf_op jit(solution)/shard_map/reduce_scatter | solution.py:45
  218.3 0.0 all-reduce.2.cloned.1.call-update
  218.3 29.1 %convolution_convert_fusion = bf16[1,128,4096]{2,0,1:T(2,128)(2,1)S(1)} fusion(bf16[1,255,4096]{2,1,0:T(8,128)(2,1)S(1)} %copy-done.2, bf16[128,1,4096]{2,0,1:T(8,128)(2,1)} %dynamic-slice_bitcast_fusion), kind=kOutput, calls=%fused_computation | convolution fusion | flops 134742016 | bytes 4186112 | tf_op jit(solution)/shard_map/conv_general_dilated | solution.py:17
  247.5 2.1 copy.12
  249.6 1.6 broadcast_multiply_fusion
  (57 shorter events, 0.2 us)
Async XLA Ops:
  7.2 114.5 %copy-start = (bf16[1,128,4096]{2,1,0:T(8,128)(2,1)S(1)}, bf16[1,128,4096]{2,1,0:T(8,128)(2,1)}, u32[]{:S(2)}) copy-start(bf16[1,128,4096]{2,1,0:T(8,128)(2,1)} %param.4) | copy-start | bytes 3145732
  7.2 211.1 %reduce-scatter.2.cloned.1.call-start = ((), (), s32[]{:S(2)}) async-start(), calls=%async_computation.1 | async-start | bytes 2228224 | tf_op jit(solution)/shard_map/reduce_scatter | solution.py:45
  7.2 7.7 %collective-permute-start.1 = (bf16[8,4096]{1,0:T(8,128)(2,1)}, bf16[8,4096]{1,0:T(8,128)(2,1)S(1)}, u32[]{:S(2)}, u32[]{:S(2)}) collective-permute-start(bf16[8,4096]{1,0:T(8,128)(2,1)} %param.7), channel_id=1, source_target_pairs={{0,2},{2,4},{4,6},{6,8},{8,10},{10,12},{12,14},{14,16},{16,18},{18... | collective-permute-start | bytes 196616 | tf_op jit(solution)/shard_map/ppermute | solution.py:39
  14.9 6.4 %collective-permute-start.2 = (bf16[8,4096]{1,0:T(8,128)(2,1)S(1)}, bf16[8,4096]{1,0:T(8,128)(2,1)S(1)}, u32[]{:S(2)}, u32[]{:S(2)}) collective-permute-start(bf16[8,4096]{1,0:T(8,128)(2,1)S(1)} %collective-permute-done.1), channel_id=1, source_target_pairs={{0,2},{2,4},{4,6},{6,8},{8,10},{10,12},{12,14},{14,16},{16,18},{18... | collective-permute-start | bytes 196616 | tf_op jit(solution)/shard_map/ppermute | solution.py:39
  21.3 6.4 %collective-permute-start.3 = (bf16[8,4096]{1,0:T(8,128)(2,1)S(1)}, bf16[8,4096]{1,0:T(8,128)(2,1)S(1)}, u32[]{:S(2)}, u32[]{:S(2)}) collective-permute-start(bf16[8,4096]{1,0:T(8,128)(2,1)S(1)} %collective-permute-done.2), channel_id=1, source_target_pairs={{0,2},{2,4},{4,6},{6,8},{8,10},{10,12},{12,14},{14,16},{16,18},{18... | collective-permute-start | bytes 196616 | tf_op jit(solution)/shard_map/ppermute | solution.py:39
  27.7 6.4 %collective-permute-start.4 = (bf16[8,4096]{1,0:T(8,128)(2,1)S(1)}, bf16[8,4096]{1,0:T(8,128)(2,1)S(1)}, u32[]{:S(2)}, u32[]{:S(2)}) collective-permute-start(bf16[8,4096]{1,0:T(8,128)(2,1)S(1)} %collective-permute-done.3), channel_id=1, source_target_pairs={{0,2},{2,4},{4,6},{6,8},{8,10},{10,12},{12,14},{14,16},{16,18},{18... | collective-permute-start | bytes 196616 | tf_op jit(solution)/shard_map/ppermute | solution.py:39
  34.1 6.4 %collective-permute-start.5 = (bf16[8,4096]{1,0:T(8,128)(2,1)S(1)}, bf16[8,4096]{1,0:T(8,128)(2,1)S(1)}, u32[]{:S(2)}, u32[]{:S(2)}) collective-permute-start(bf16[8,4096]{1,0:T(8,128)(2,1)S(1)} %collective-permute-done.4), channel_id=1, source_target_pairs={{0,2},{2,4},{4,6},{6,8},{8,10},{10,12},{12,14},{14,16},{16,18},{18... | collective-permute-start | bytes 196616 | tf_op jit(solution)/shard_map/ppermute | solution.py:39
  40.5 6.4 %collective-permute-start.6 = (bf16[8,4096]{1,0:T(8,128)(2,1)S(1)}, bf16[8,4096]{1,0:T(8,128)(2,1)S(1)}, u32[]{:S(2)}, u32[]{:S(2)}) collective-permute-start(bf16[8,4096]{1,0:T(8,128)(2,1)S(1)} %collective-permute-done.5), channel_id=1, source_target_pairs={{0,2},{2,4},{4,6},{6,8},{8,10},{10,12},{12,14},{14,16},{16,18},{18... | collective-permute-start | bytes 196616 | tf_op jit(solution)/shard_map/ppermute | solution.py:39
  46.9 44.9 %copy-start.5 = (bf16[8,4096]{1,0:T(8,128)(2,1)}, bf16[8,4096]{1,0:T(8,128)(2,1)S(1)}, u32[]{:S(2)}) copy-start(bf16[8,4096]{1,0:T(8,128)(2,1)S(1)} %collective-permute-done.6) | copy-start | bytes 196612
  46.9 6.4 %collective-permute-start.7 = (bf16[8,4096]{1,0:T(8,128)(2,1)S(1)}, bf16[8,4096]{1,0:T(8,128)(2,1)S(1)}, u32[]{:S(2)}, u32[]{:S(2)}) collective-permute-start(bf16[8,4096]{1,0:T(8,128)(2,1)S(1)} %collective-permute-done.6), channel_id=1, source_target_pairs={{0,2},{2,4},{4,6},{6,8},{8,10},{10,12},{12,14},{14,16},{16,18},{18... | collective-permute-start | bytes 196616 | tf_op jit(solution)/shard_map/ppermute | solution.py:39
  53.2 38.3 %copy-start.7 = (bf16[8,4096]{1,0:T(8,128)(2,1)}, bf16[8,4096]{1,0:T(8,128)(2,1)S(1)}, u32[]{:S(2)}) copy-start(bf16[8,4096]{1,0:T(8,128)(2,1)S(1)} %collective-permute-done.7) | copy-start | bytes 196612
  53.2 6.4 %collective-permute-start.8 = (bf16[8,4096]{1,0:T(8,128)(2,1)S(1)}, bf16[8,4096]{1,0:T(8,128)(2,1)S(1)}, u32[]{:S(2)}, u32[]{:S(2)}) collective-permute-start(bf16[8,4096]{1,0:T(8,128)(2,1)S(1)} %collective-permute-done.7), channel_id=1, source_target_pairs={{0,2},{2,4},{4,6},{6,8},{8,10},{10,12},{12,14},{14,16},{16,18},{18... | collective-permute-start | bytes 196616 | tf_op jit(solution)/shard_map/ppermute | solution.py:39
  59.6 32.0 %copy-start.9 = (bf16[8,4096]{1,0:T(8,128)(2,1)}, bf16[8,4096]{1,0:T(8,128)(2,1)S(1)}, u32[]{:S(2)}) copy-start(bf16[8,4096]{1,0:T(8,128)(2,1)S(1)} %collective-permute-done.8) | copy-start | bytes 196612
  59.6 6.4 %collective-permute-start.9 = (bf16[8,4096]{1,0:T(8,128)(2,1)S(1)}, bf16[8,4096]{1,0:T(8,128)(2,1)S(1)}, u32[]{:S(2)}, u32[]{:S(2)}) collective-permute-start(bf16[8,4096]{1,0:T(8,128)(2,1)S(1)} %collective-permute-done.8), channel_id=1, source_target_pairs={{0,2},{2,4},{4,6},{6,8},{8,10},{10,12},{12,14},{14,16},{16,18},{18... | collective-permute-start | bytes 196616 | tf_op jit(solution)/shard_map/ppermute | solution.py:39
  66.0 25.6 %copy-start.11 = (bf16[8,4096]{1,0:T(8,128)(2,1)}, bf16[8,4096]{1,0:T(8,128)(2,1)S(1)}, u32[]{:S(2)}) copy-start(bf16[8,4096]{1,0:T(8,128)(2,1)S(1)} %collective-permute-done.9) | copy-start | bytes 196612
  66.0 6.4 %collective-permute-start.10 = (bf16[8,4096]{1,0:T(8,128)(2,1)S(1)}, bf16[8,4096]{1,0:T(8,128)(2,1)S(1)}, u32[]{:S(2)}, u32[]{:S(2)}) collective-permute-start(bf16[8,4096]{1,0:T(8,128)(2,1)S(1)} %collective-permute-done.9), channel_id=1, source_target_pairs={{0,2},{2,4},{4,6},{6,8},{8,10},{10,12},{12,14},{14,16},{16,18},{18... | collective-permute-start | bytes 196616 | tf_op jit(solution)/shard_map/ppermute | solution.py:39
  72.4 19.2 %copy-start.13 = (bf16[8,4096]{1,0:T(8,128)(2,1)}, bf16[8,4096]{1,0:T(8,128)(2,1)S(1)}, u32[]{:S(2)}) copy-start(bf16[8,4096]{1,0:T(8,128)(2,1)S(1)} %collective-permute-done.10) | copy-start | bytes 196612
  72.4 6.4 %collective-permute-start.11 = (bf16[8,4096]{1,0:T(8,128)(2,1)S(1)}, bf16[8,4096]{1,0:T(8,128)(2,1)S(1)}, u32[]{:S(2)}, u32[]{:S(2)}) collective-permute-start(bf16[8,4096]{1,0:T(8,128)(2,1)S(1)} %collective-permute-done.10), channel_id=1, source_target_pairs={{0,2},{2,4},{4,6},{6,8},{8,10},{10,12},{12,14},{14,16},{16,18},{18... | collective-permute-start | bytes 196616 | tf_op jit(solution)/shard_map/ppermute | solution.py:39
  78.8 12.8 %copy-start.15 = (bf16[8,4096]{1,0:T(8,128)(2,1)}, bf16[8,4096]{1,0:T(8,128)(2,1)S(1)}, u32[]{:S(2)}) copy-start(bf16[8,4096]{1,0:T(8,128)(2,1)S(1)} %collective-permute-done.11) | copy-start | bytes 196612
  78.8 6.4 %collective-permute-start.12 = (bf16[8,4096]{1,0:T(8,128)(2,1)S(1)}, bf16[8,4096]{1,0:T(8,128)(2,1)S(1)}, u32[]{:S(2)}, u32[]{:S(2)}) collective-permute-start(bf16[8,4096]{1,0:T(8,128)(2,1)S(1)} %collective-permute-done.11), channel_id=1, source_target_pairs={{0,2},{2,4},{4,6},{6,8},{8,10},{10,12},{12,14},{14,16},{16,18},{18... | collective-permute-start | bytes 196616 | tf_op jit(solution)/shard_map/ppermute | solution.py:39
  85.2 6.4 %copy-start.17 = (bf16[8,4096]{1,0:T(8,128)(2,1)}, bf16[8,4096]{1,0:T(8,128)(2,1)S(1)}, u32[]{:S(2)}) copy-start(bf16[8,4096]{1,0:T(8,128)(2,1)S(1)} %collective-permute-done.12) | copy-start | bytes 196612
  85.2 6.4 %collective-permute-start.13 = (bf16[8,4096]{1,0:T(8,128)(2,1)S(1)}, bf16[8,4096]{1,0:T(8,128)(2,1)S(1)}, u32[]{:S(2)}, u32[]{:S(2)}) collective-permute-start(bf16[8,4096]{1,0:T(8,128)(2,1)S(1)} %collective-permute-done.12), channel_id=1, source_target_pairs={{0,2},{2,4},{4,6},{6,8},{8,10},{10,12},{12,14},{14,16},{16,18},{18... | collective-permute-start | bytes 196616 | tf_op jit(solution)/shard_map/ppermute | solution.py:39
  91.6 6.7 %copy-start.19 = (bf16[8,4096]{1,0:T(8,128)(2,1)}, bf16[8,4096]{1,0:T(8,128)(2,1)S(1)}, u32[]{:S(2)}) copy-start(bf16[8,4096]{1,0:T(8,128)(2,1)S(1)} %collective-permute-done.13) | copy-start | bytes 196612
  91.6 6.5 %collective-permute-start.14 = (bf16[8,4096]{1,0:T(8,128)(2,1)S(1)}, bf16[8,4096]{1,0:T(8,128)(2,1)}, u32[]{:S(2)}, u32[]{:S(2)}) collective-permute-start(bf16[8,4096]{1,0:T(8,128)(2,1)S(1)} %collective-permute-done.13), channel_id=1, source_target_pairs={{0,2},{2,4},{4,6},{6,8},{8,10},{10,12},{12,14},{14,16},{16,18},{18... | collective-permute-start | bytes 196616 | tf_op jit(solution)/shard_map/ppermute | solution.py:39
  93.5 19.9 %copy-start.4 = (bf16[8,4096]{1,0:T(8,128)(2,1)S(1)}, bf16[8,4096]{1,0:T(8,128)(2,1)}, u32[]{:S(2)}) copy-start(bf16[8,4096]{1,0:T(8,128)(2,1)} %param.7) | copy-start | bytes 196612
  98.2 6.7 %collective-permute-start.15 = (bf16[8,4096]{1,0:T(8,128)(2,1)}, bf16[8,4096]{1,0:T(8,128)(2,1)}, u32[]{:S(2)}, u32[]{:S(2)}) collective-permute-start(bf16[8,4096]{1,0:T(8,128)(2,1)} %collective-permute-done.14), channel_id=1, source_target_pairs={{0,2},{2,4},{4,6},{6,8},{8,10},{10,12},{12,14},{14,16},{16,18},{18... | collective-permute-start | bytes 196616 | tf_op jit(solution)/shard_map/ppermute | solution.py:39
  98.3 22.0 %collective-permute-start = (bf16[127,4096]{1,0:T(8,128)(2,1)S(1)}, bf16[127,4096]{1,0:T(8,128)(2,1)}, u32[]{:S(2)}, u32[]{:S(2)}) collective-permute-start(bf16[127,4096]{1,0:T(8,128)(2,1)S(1)} %slice_bitcast_fusion), channel_id=1, source_target_pairs={{1,0},{3,2},{5,4},{7,6},{9,8},{11,10},{13,12},{15,14},{17,16},{19,... | collective-permute-start | bytes 3121160 | tf_op jit(solution)/shard_map/ppermute | solution.py:13
  99.6 15.5 %copy-start.20 = (bf16[8,4096]{1,0:T(8,128)(2,1)S(1)}, bf16[8,4096]{1,0:T(8,128)(2,1)}, u32[]{:S(2)}) copy-start(bf16[8,4096]{1,0:T(8,128)(2,1)} %copy-done.19) | copy-start | bytes 196612
  99.6 15.5 %copy-start.18 = (bf16[8,4096]{1,0:T(8,128)(2,1)S(1)}, bf16[8,4096]{1,0:T(8,128)(2,1)}, u32[]{:S(2)}) copy-start(bf16[8,4096]{1,0:T(8,128)(2,1)} %copy-done.17) | copy-start | bytes 196612
  99.6 15.5 %copy-start.16 = (bf16[8,4096]{1,0:T(8,128)(2,1)S(1)}, bf16[8,4096]{1,0:T(8,128)(2,1)}, u32[]{:S(2)}) copy-start(bf16[8,4096]{1,0:T(8,128)(2,1)} %copy-done.15) | copy-start | bytes 196612
  99.7 15.5 %copy-start.14 = (bf16[8,4096]{1,0:T(8,128)(2,1)S(1)}, bf16[8,4096]{1,0:T(8,128)(2,1)}, u32[]{:S(2)}) copy-start(bf16[8,4096]{1,0:T(8,128)(2,1)} %copy-done.13) | copy-start | bytes 196612
  99.7 15.5 %copy-start.12 = (bf16[8,4096]{1,0:T(8,128)(2,1)S(1)}, bf16[8,4096]{1,0:T(8,128)(2,1)}, u32[]{:S(2)}) copy-start(bf16[8,4096]{1,0:T(8,128)(2,1)} %copy-done.11) | copy-start | bytes 196612
  99.7 15.6 %copy-start.10 = (bf16[8,4096]{1,0:T(8,128)(2,1)S(1)}, bf16[8,4096]{1,0:T(8,128)(2,1)}, u32[]{:S(2)}) copy-start(bf16[8,4096]{1,0:T(8,128)(2,1)} %copy-done.9) | copy-start | bytes 196612
  99.7 15.6 %copy-start.8 = (bf16[8,4096]{1,0:T(8,128)(2,1)S(1)}, bf16[8,4096]{1,0:T(8,128)(2,1)}, u32[]{:S(2)}) copy-start(bf16[8,4096]{1,0:T(8,128)(2,1)} %copy-done.7) | copy-start | bytes 196612
  99.7 15.6 %copy-start.6 = (bf16[8,4096]{1,0:T(8,128)(2,1)S(1)}, bf16[8,4096]{1,0:T(8,128)(2,1)}, u32[]{:S(2)}) copy-start(bf16[8,4096]{1,0:T(8,128)(2,1)} %copy-done.5) | copy-start | bytes 196612
  115.3 5.0 %copy-start.3 = (bf16[256,4096]{1,0:T(8,128)(2,1)}, bf16[256,4096]{1,0:T(8,128)(2,1)S(1)}, u32[]{:S(2)}) copy-start(bf16[256,4096]{1,0:T(8,128)(2,1)S(1)} %constant_dynamic-update-slice_fusion.6) | copy-start | bytes 6291460
  121.7 30.1 %copy-start.1 = (bf16[1,255,4096]{2,1,0:T(8,128)(2,1)}, bf16[1,255,4096]{2,1,0:T(8,128)(2,1)S(1)}, u32[]{:S(2)}) copy-start(bf16[1,255,4096]{2,1,0:T(8,128)(2,1)S(1)} %maximum_bitcast_fusion) | copy-start | bytes 6266884
  154.8 63.5 %copy-start.2 = (bf16[1,255,4096]{2,1,0:T(8,128)(2,1)S(1)}, bf16[1,255,4096]{2,1,0:T(8,128)(2,1)}, u32[]{:S(2)}) copy-start(bf16[1,255,4096]{2,1,0:T(8,128)(2,1)} %copy-done.1) | copy-start | bytes 6266884
  154.8 94.7 %all-reduce.2.cloned.1.call-start = ((), (), s32[]{:S(2)}) async-start(), calls=%async_computation.2 | async-start | bytes 262144 | tf_op jit(solution)/shard_map/psum | solution.py:44
Sparse Core Ops, SparseCore 0:
  155.0 63.3 reduce-scatter.1
  220.6 20.4 all-reduce.1
